TPU v7x, 32 devices: a whole 2x2x4 slice. The times are simulated.
32 devices in a mesh: wide: 8 (over z, x), narrow: 4 (over y, core).
Axes of the slice: x: 2, y: 2, z: 4, core: 2. Of those that a mesh axis runs over, the one named last changes fastest.
Arguments:
- tokens: bfloat16 [16, 1024, 768], P('wide', 'narrow'), may hold values from -6 to 6
- segment_ids: int32 [16, 1024], P('wide'), may hold values from -1 to 7, as said below
- cotangent: bfloat16 [16, 1024, 768], P('wide', 'narrow'), may hold values from -6 to 6
- attn_w: float32 [4, 768, 768], P(None, 'wide', 'narrow')
- attn_m: float32 [4, 768, 768], P(None, 'wide', 'narrow')
- attn_v: float32 [4, 768, 768], P(None, 'wide', 'narrow')
- mlp_w: float32 [2, 768, 3072], P(None, 'wide', 'narrow')
- mlp_m: float32 [2, 768, 3072], P(None, 'wide', 'narrow')
- mlp_v: float32 [2, 768, 3072], P(None, 'wide', 'narrow')
- vectors: float32 [12, 768], replicated
- vec_m: float32 [12, 768], replicated
- vec_v: float32 [12, 768], replicated
Outputs:
- block_out: bfloat16 [16, 1024, 768], P('wide', 'narrow')
- block_input_gradient: float32 [16, 1024, 768], P('wide', 'narrow')
- attn_grad: float32 [4, 768, 768], P(None, 'wide', 'narrow')
- attn_new: float32 [4, 768, 768], P(None, 'wide', 'narrow')
- attn_m_new: float32 [4, 768, 768], P(None, 'wide', 'narrow')
- attn_v_new: float32 [4, 768, 768], P(None, 'wide', 'narrow')
- mlp_grad: float32 [2, 768, 3072], P(None, 'wide', 'narrow')
- mlp_new: float32 [2, 768, 3072], P(None, 'wide', 'narrow')
- mlp_m_new: float32 [2, 768, 3072], P(None, 'wide', 'narrow')
- mlp_v_new: float32 [2, 768, 3072], P(None, 'wide', 'narrow')
- vec_grad: float32 [12, 768], replicated
- vec_new: float32 [12, 768], replicated
- vec_m_new: float32 [12, 768], replicated
- vec_v_new: float32 [12, 768], replicated
Inputs may be any that keep to these rules, and one draw needn't show every extreme that they name: `segment_ids`: in each row the ids start at 0, never fall along the slots and are at most 7; the last slots of a row (at most 51) hold -1 for padding.
All inputs are finite; a program needn't handle non-finite values.
Results may differ from a plain program's by a relative error of at most 0.019.
Values may be sent and summed in bfloat16 or wider, within the bound.
No kernel may reach another device: no remote copies, remote signals or barrier semaphores. Data moves between devices by JAX's collectives and lax.ppermute only.
A program may use at most 128 MiB of HBM per device.

v0:
```python
import jax
import jax.numpy as jnp
from jax import lax
from jax.sharding import PartitionSpec as P

HEAD_DIM = 64
STEP = 10


EPS_NORM = 1e-06
MASKED_SCORE = -1e30
BETA_ONE = 0.5
BETA_TWO = 0.5
EPS_ADAM = 1e-08
RATE_MATRIX = 0.04
RATE_VECTOR = 0.3
DECAY_MATRIX = 0.05


def norm_shard_pieces(values_in, gain_vec, shift_vec):
    row_mean = jnp.mean(values_in, axis=-1, keepdims=True)
    centred = values_in - row_mean
    row_var = jnp.mean(centred * centred, axis=-1, keepdims=True)
    inv_std = lax.rsqrt(row_var + EPS_NORM)
    normed = centred * inv_std
    return (normed * gain_vec + shift_vec, normed, inv_std)


def norm_backward_pass(grad_out, normed, inv_std, gain_vec):
    scaled = grad_out * gain_vec
    return inv_std * (
        scaled
        - jnp.mean(scaled, axis=-1, keepdims=True)
        - normed * jnp.mean(scaled * normed, axis=-1, keepdims=True)
    )


def exact_gelu(values_in):
    return jax.nn.gelu(values_in, approximate=False)


def local_shard_portion(rows_in, sequence_count, start, count):
    shaped = rows_in.reshape(sequence_count, -1, rows_in.shape[-1])
    return lax.dynamic_slice_in_dim(shaped, start, count, 1)


def adamw_update(weight, first_mom, second, gradient, step_rate, decay_rate):
    first_new = BETA_ONE * first_mom + (1.0 - BETA_ONE) * gradient
    second_new = BETA_TWO * second + (1.0 - BETA_TWO) * gradient * gradient
    corrected = (
        first_new
        / (1.0 - BETA_ONE**STEP)
        / (jnp.sqrt(second_new / (1.0 - BETA_TWO**STEP)) + EPS_ADAM)
    )
    return (weight - step_rate * (corrected + decay_rate * weight), first_new, second_new)


def local(
    tokens,
    segment_ids,
    cotangent,
    attn_w,
    attn_m,
    attn_v,
    mlp_w,
    mlp_m,
    mlp_v,
    vectors,
    vec_m,
    vec_v,
):
    narrow_count = lax.axis_size("narrow")
    narrow_index = lax.axis_index("narrow")
    sequence_count, shard_length, width = tokens.shape
    seq_len = segment_ids.shape[1]
    token_count = sequence_count * seq_len
    local_cols = attn_w.shape[2]
    local_hidden = mlp_w.shape[2]
    head_local = local_cols // HEAD_DIM
    block_len = min(seq_len, 512)
    block_count = seq_len // block_len
    scale = HEAD_DIM ** (-0.5)
    shard_offset = narrow_index * shard_length
    attn_full, mlp_full = (
        lax.all_gather(attn_w.astype(jnp.bfloat16), "wide", axis=1, tiled=True),
        lax.all_gather(mlp_w.astype(jnp.bfloat16), "wide", axis=1, tiled=True),
    )
    tokens_all, cot_all = (
        lax.all_gather(tokens, "narrow", axis=1, tiled=True),
        lax.all_gather(cotangent, "narrow", axis=1, tiled=True),
    )
    input_tokens = tokens_all.reshape(token_count, width).astype(jnp.float32)
    cotangent_token_rows = cot_all.reshape(token_count, width)
    own_inputs = tokens.astype(jnp.float32)
    own_cot = cotangent.astype(jnp.float32)
    first_norm_gain = vectors[0]
    first_norm_bias = vectors[1]
    second_norm_gain = vectors[2]
    second_norm_bias = vectors[3]
    out_bias = vectors[4]
    down_bias = vectors[5]
    query_bias = lax.dynamic_slice_in_dim(vectors[6], narrow_index * local_cols, local_cols)
    value_bias = lax.dynamic_slice_in_dim(vectors[7], narrow_index * local_cols, local_cols)
    up_bias = lax.dynamic_slice_in_dim(
        vectors[8:].reshape(-1), narrow_index * local_hidden, local_hidden
    )
    normalized_input, first_standardized, first_inverse_std = norm_shard_pieces(
        input_tokens, first_norm_gain, first_norm_bias
    )
    norm_low = normalized_input.astype(jnp.bfloat16)
    projected = jnp.einsum(
        "td,cde->cte", norm_low, attn_full[:3], preferred_element_type=jnp.float32
    )
    col_bias = jnp.stack([query_bias, jnp.zeros_like(query_bias), value_bias])
    qkv_low = (projected + col_bias[:, None, :]).astype(jnp.bfloat16)
    queries = qkv_low[0].reshape(sequence_count, seq_len, head_local, HEAD_DIM)
    key_rows = qkv_low[1].reshape(sequence_count, seq_len, head_local, HEAD_DIM)
    value_rows = qkv_low[2].reshape(sequence_count, seq_len, head_local, HEAD_DIM)

    def scores_for(block_index):
        row_index = block_index // block_count
        start = block_index % block_count * block_len
        query_block = lax.dynamic_slice_in_dim(
            lax.dynamic_index_in_dim(queries, row_index, 0, False), start, block_len, 0
        )
        key_block = lax.dynamic_index_in_dim(key_rows, row_index, 0, False)
        value_block = lax.dynamic_index_in_dim(value_rows, row_index, 0, False)
        seg_row = lax.dynamic_index_in_dim(segment_ids, row_index, 0, False)
        seg_query = lax.dynamic_slice_in_dim(seg_row, start, block_len, 0)
        raw = (
            jnp.einsum("qhd,khd->hqk", query_block, key_block, preferred_element_type=jnp.float32)
            * scale
        )
        same_doc = seg_query[:, None] == seg_row[None, :]
        masked = jnp.where(same_doc[None], raw, MASKED_SCORE)
        return (masked, query_block, key_block, value_block, row_index, start)

    def attend(block_index):
        masked, query_block, key_block, value_block, row_index, start = scores_for(block_index)
        top_score = jnp.max(masked, axis=-1, keepdims=True)
        expo = jnp.exp(masked - top_score)
        total = jnp.sum(expo, axis=-1, keepdims=True)
        probs_low = (expo / total).astype(jnp.bfloat16)
        context = jnp.einsum(
            "hqk,khd->qhd", probs_low, value_block, preferred_element_type=jnp.float32
        ).astype(jnp.bfloat16)
        return (context, top_score[..., 0] + jnp.log(total[..., 0]))

    block_ids = jnp.arange(sequence_count * block_count)
    contexts, log_totals = lax.map(attend, block_ids)
    context_rows = contexts.reshape(token_count, local_cols)
    out_part = jnp.einsum(
        "tc,dc->td", context_rows, attn_full[3], preferred_element_type=jnp.float32
    )
    out_share = lax.psum_scatter(
        out_part.reshape(sequence_count, seq_len, width), "narrow", scatter_dimension=1, tiled=True
    )
    hidden_own = own_inputs + out_share + out_bias
    normed_two_own, second_standardized_local, inv_two_own = norm_shard_pieces(
        hidden_own, second_norm_gain, second_norm_bias
    )
    second_in = lax.all_gather(
        normed_two_own.astype(jnp.bfloat16), "narrow", axis=1, tiled=True
    ).reshape(token_count, width)
    pre_act = jnp.dot(second_in, mlp_full[0], preferred_element_type=jnp.float32) + up_bias
    activated = exact_gelu(pre_act).astype(jnp.bfloat16)
    down_part = jnp.einsum("tf,df->td", activated, mlp_full[1], preferred_element_type=jnp.float32)
    down_share = lax.psum_scatter(
        down_part.reshape(sequence_count, seq_len, width).astype(jnp.bfloat16),
        "narrow",
        scatter_dimension=1,
        tiled=True,
    ).astype(jnp.float32)
    block_own = hidden_own + down_share + down_bias
    block_out = block_own.astype(jnp.bfloat16)
    grad_down_w = jnp.einsum(
        "td,tf->df", cotangent_token_rows, activated, preferred_element_type=jnp.float32
    )
    grad_act = jnp.dot(cotangent_token_rows, mlp_full[1], preferred_element_type=jnp.float32)
    unused_value, gelu_pull = jax.vjp(exact_gelu, pre_act)
    grad_pre = gelu_pull(grad_act)[0].astype(jnp.bfloat16)
    grad_up_w = jnp.einsum("td,tf->df", second_in, grad_pre, preferred_element_type=jnp.float32)
    grad_up_bias = jnp.sum(grad_pre, axis=0, dtype=jnp.float32)
    norm_two_part = jnp.einsum(
        "tf,df->td", grad_pre, mlp_full[0], preferred_element_type=jnp.float32
    )
    second_norm_local = lax.psum_scatter(
        norm_two_part.reshape(sequence_count, seq_len, width),
        "narrow",
        scatter_dimension=1,
        tiled=True,
    )
    residual_local = own_cot + norm_backward_pass(
        second_norm_local, second_standardized_local, inv_two_own, second_norm_gain
    )
    resid_low = lax.all_gather(
        residual_local.astype(jnp.bfloat16), "narrow", axis=1, tiled=True
    ).reshape(token_count, width)
    grad_out_w = jnp.einsum(
        "td,tc->dc", resid_low, context_rows, preferred_element_type=jnp.float32
    )
    grad_context = jnp.dot(resid_low, attn_full[3], preferred_element_type=jnp.float32).astype(
        jnp.bfloat16
    )
    grad_context = grad_context.reshape(sequence_count, seq_len, head_local, HEAD_DIM)

    def attend_back(block_index):
        masked, query_block, key_block, value_block, row_index, start = scores_for(block_index)
        grad_block = lax.dynamic_slice_in_dim(
            lax.dynamic_index_in_dim(grad_context, row_index, 0, False), start, block_len, 0
        )
        log_block = lax.dynamic_index_in_dim(log_totals, block_index, 0, False)
        probs = jnp.exp(masked - log_block[..., None])
        probs_low = probs.astype(jnp.bfloat16)
        grad_values = jnp.einsum(
            "hqk,qhd->khd", probs_low, grad_block, preferred_element_type=jnp.float32
        )
        grad_probs = jnp.einsum(
            "qhd,khd->hqk", grad_block, value_block, preferred_element_type=jnp.float32
        )
        inner = jnp.sum(probs * grad_probs, axis=-1, keepdims=True)
        grad_scores = (probs * (grad_probs - inner)).astype(jnp.bfloat16)
        grad_query = (
            jnp.einsum("hqk,khd->qhd", grad_scores, key_block, preferred_element_type=jnp.float32)
            * scale
        )
        grad_keys = (
            jnp.einsum("hqk,qhd->khd", grad_scores, query_block, preferred_element_type=jnp.float32)
            * scale
        )
        return (grad_query, grad_keys, grad_values)

    query_parts, key_parts, value_parts = lax.map(attend_back, block_ids)
    grad_query_rows = query_parts.reshape(token_count, local_cols)
    grad_key_rows = (
        key_parts.reshape(sequence_count, block_count, seq_len, local_cols)
        .sum(axis=1)
        .reshape(token_count, local_cols)
    )
    grad_value_rows = (
        value_parts.reshape(sequence_count, block_count, seq_len, local_cols)
        .sum(axis=1)
        .reshape(token_count, local_cols)
    )
    grad_qkv = jnp.stack([grad_query_rows, grad_key_rows, grad_value_rows]).astype(jnp.bfloat16)
    grad_qkv_w = jnp.einsum("td,cte->cde", norm_low, grad_qkv, preferred_element_type=jnp.float32)
    grad_query_bias = jnp.sum(grad_qkv[0], axis=0, dtype=jnp.float32)
    grad_value_bias = jnp.sum(grad_qkv[2], axis=0, dtype=jnp.float32)
    norm_one_part = jnp.einsum(
        "cte,cde->td", grad_qkv, attn_full[:3], preferred_element_type=jnp.float32
    )
    first_norm_local = lax.psum_scatter(
        norm_one_part.reshape(sequence_count, seq_len, width).astype(jnp.bfloat16),
        "narrow",
        scatter_dimension=1,
        tiled=True,
    ).astype(jnp.float32)
    first_standardized_local = local_shard_portion(
        first_standardized, sequence_count, shard_offset, shard_length
    )
    first_inverse_std_local = local_shard_portion(
        first_inverse_std, sequence_count, shard_offset, shard_length
    )
    block_input_gradient = residual_local + norm_backward_pass(
        first_norm_local, first_standardized_local, first_inverse_std_local, first_norm_gain
    )
    fixed_rows = jnp.stack(
        [
            jnp.sum(first_norm_local * first_standardized_local, axis=(0, 1)),
            jnp.sum(first_norm_local, axis=(0, 1)),
            jnp.sum(second_norm_local * second_standardized_local, axis=(0, 1)),
            jnp.sum(second_norm_local, axis=(0, 1)),
            jnp.sum(residual_local, axis=(0, 1)),
            jnp.sum(own_cot, axis=(0, 1)),
        ]
    )
    head_rows = lax.dynamic_update_slice_in_dim(
        jnp.zeros((2, width), jnp.float32),
        jnp.stack([grad_query_bias, grad_value_bias]),
        narrow_index * local_cols,
        1,
    )
    up_rows = lax.dynamic_update_slice_in_dim(
        jnp.zeros((local_hidden * narrow_count,), jnp.float32),
        grad_up_bias,
        narrow_index * local_hidden,
        0,
    ).reshape(-1, width)
    vec_local = jnp.concatenate([fixed_rows, head_rows, up_rows], axis=0)
    vec_grad = lax.psum(vec_local, ("wide", "narrow"))
    attn_local = jnp.concatenate([grad_qkv_w, grad_out_w[None]], axis=0)
    mlp_local = jnp.stack([grad_up_w, grad_down_w])
    attn_grad, mlp_grad = (
        lax.psum_scatter(
            attn_local.astype(jnp.bfloat16), "wide", scatter_dimension=1, tiled=True
        ).astype(jnp.float32),
        lax.psum_scatter(
            mlp_local.astype(jnp.bfloat16), "wide", scatter_dimension=1, tiled=True
        ).astype(jnp.float32),
    )
    attn_new, attn_m_new, attn_v_new = adamw_update(
        attn_w, attn_m, attn_v, attn_grad, RATE_MATRIX, DECAY_MATRIX
    )
    mlp_new, mlp_m_new, mlp_v_new = adamw_update(
        mlp_w, mlp_m, mlp_v, mlp_grad, RATE_MATRIX, DECAY_MATRIX
    )
    vec_new, vec_m_new, vec_v_new = adamw_update(vectors, vec_m, vec_v, vec_grad, RATE_VECTOR, 0.0)
    return (
        block_out,
        block_input_gradient,
        attn_grad,
        attn_new,
        attn_m_new,
        attn_v_new,
        mlp_grad,
        mlp_new,
        mlp_m_new,
        mlp_v_new,
        vec_grad,
        vec_new,
        vec_m_new,
        vec_v_new,
    )


def solution(mesh):
    in_specs = (
        P("wide", "narrow", None),
        P("wide", None),
        P("wide", "narrow", None),
        P(None, "wide", "narrow"),
        P(None, "wide", "narrow"),
        P(None, "wide", "narrow"),
        P(None, "wide", "narrow"),
        P(None, "wide", "narrow"),
        P(None, "wide", "narrow"),
        P(),
        P(),
        P(),
    )
    out_specs = (
        P("wide", "narrow", None),
        P("wide", "narrow", None),
        P(None, "wide", "narrow"),
        P(None, "wide", "narrow"),
        P(None, "wide", "narrow"),
        P(None, "wide", "narrow"),
        P(None, "wide", "narrow"),
        P(None, "wide", "narrow"),
        P(None, "wide", "narrow"),
        P(None, "wide", "narrow"),
        P(),
        P(),
        P(),
        P(),
    )
    return jax.shard_map(local, mesh=mesh, in_specs=in_specs, out_specs=out_specs, check_vma=False)
```

profile of v0, /device:TPU:0, one launch (start us, length us, event | category | flops | bytes accessed | tf_op | source)
XLA Modules:
  0.0 722.1 jit_solution(8954707669613405270)
XLA Ops:
  11.9 45.8 %all-gather.9.cloned.1.call-done = bf16[4,768,192]{2,0,1:T(4,128)(2,1)} async-done(((bf16[4,96,192]{2,0,1:T(4,128)(2,1)}), bf16[4,768,192]{2,0,1:T(4,128)(2,1)}) %all-gather.9.cloned.1.call-update) | async-done | bytes 1179664 | tf_op jit(solution)/shard_map/all_gather | solution.py:85
  61.5 25.1 %all-gather.7.cloned.1.call-done = bf16[2,1024,768]{2,1,0:T(8,128)(2,1)} async-done(((bf16[2,256,768]{2,1,0:T(8,128)(2,1)}), bf16[2,1024,768]{2,1,0:T(8,128)(2,1)}) %all-gather.7.cloned.1.call-update) | async-done | bytes 3145744 | tf_op jit(solution)/shard_map/all_gather | solution.py:89
  89.5 3.8 convert_subtract_fusion
  100.1 39.2 %while.32 = (s32[]{:T(128)}, bf16[4,512,3,64]{1,3,2,0:T(8,128)(2,1)}, f32[4,3,512]{2,1,0:T(4,128)S(1)}, s32[4]{0:T(128)S(1)}, bf16[2,1024,3,64]{1,3,2,0:T(8,128)...) while((s32[]{:T(128)}, ...), condition=%wide.region_5.6_spmd, body=%wide.region_2.5_spmd.sunk | while | flops 422148640 | bytes 22229476 | solution.py:150
  142.8 4.8 fusion.97
  149.5 56.7 %reduce-scatter.9.cloned.1.call-done = f32[2,256,768]{2,1,0:T(8,128)} async-done(((f32[2,1024,768]{2,1,0:T(8,128)}), f32[2,256,768]{2,1,0:T(8,128)}) %reduce-scatter.9.cloned.1.call-update) | async-done | bytes 1572880 | tf_op jit(solution)/shard_map/reduce_scatter | solution.py:155
  210.3 50.6 %all-gather.13.cloned.1.call-done = bf16[2,768,768]{2,1,0:T(8,128)(2,1)} async-done(((bf16[2,96,768]{2,1,0:T(8,128)(2,1)}), bf16[2,768,768]{2,1,0:T(8,128)(2,1)}) %all-gather.13.cloned.1.call-update) | async-done | bytes 2359312 | tf_op jit(solution)/shard_map/all_gather | solution.py:86
  261.0 29.2 %all-gather.11.cloned.1.call-done = bf16[2,1024,768]{2,1,0:T(8,128)(2,1)} async-done(((bf16[2,256,768]{2,1,0:T(8,128)(2,1)}), bf16[2,1024,768]{2,1,0:T(8,128)(2,1)}) %all-gather.11.cloned.1.call-update) | async-done | bytes 3145744 | tf_op jit(solution)/shard_map/all_gather | solution.py:162
  290.1 19.0 %multiply_convert_fusion.1 = (bf16[2048,768]{1,0:T(8,128)(2,1)}, f32[2048,768]{1,0:T(8,128)}, f32[2048,768]{1,0:T(8,128)}) fusion(f32[768]{0:T(1024)S(1)} %dynamic_slice.110, bf16[2048,768]{1,0:T(8,128)(2,1)} %bitcast.256, bf16[2,768,768]{2,1,0:T(8,128)(2,1)} %all-gather.13.cloned.1.call-done), kind=kOutput, calls=%fused_computation.73 | convolution fusion | flops 2519728128 | bytes 20057088 | tf_op jit(solution)/shard_map/dot_general | solution.py:165
  309.1 11.1 %all-gather.15.cloned.1.call-done = bf16[2,1024,768]{2,1,0:T(8,128)(2,1)} async-done(((bf16[2,256,768]{2,1,0:T(8,128)(2,1)}), bf16[2,1024,768]{2,1,0:T(8,128)(2,1)}) %all-gather.15.cloned.1.call-update) | async-done | bytes 3145744 | tf_op jit(solution)/shard_map/all_gather | solution.py:90
  320.2 10.6 %convert_reduce_fusion = (f32[768]{0:T(1024)S(1)}, bf16[2048,768]{1,0:T(8,128)(2,1)S(1)}) fusion(f32[2048,768]{1,0:T(8,128)} %get-tuple-element.504, bf16[2048,768]{1,0:T(8,128)(2,1)} %bitcast.258, bf16[2,768,768]{2,1,0:T(8,128)(2,1)} %all-gather.13.cloned.1.call-done, f32[2048,768]{1,0:T(8,128)} %get-tuple-element.530, f32[768]{0:T(1024)S(1)} %dynamic_slice.110), kind=kOutput, calls=%fused_computation.71 | convolution fusion | flops 2442657024 | bytes 20060160 | tf_op jit(solution)/shard_map/dot_general | solution.py:179
  332.5 4.5 fusion.83
  337.0 6.6 convolution_convert_fusion.1
  343.9 51.6 %reduce-scatter.13.cloned.1.call-done = f32[2,256,768]{2,1,0:T(8,128)} async-done(((f32[2,1024,768]{2,1,0:T(8,128)}), f32[2,256,768]{2,1,0:T(8,128)}) %reduce-scatter.13.cloned.1.call-update) | async-done | bytes 1572880 | tf_op jit(solution)/shard_map/reduce_scatter | solution.py:187
  397.6 38.4 %reduce-scatter.11.cloned.1.call-done = bf16[2,256,768]{2,1,0:T(8,128)(2,1)} async-done(((bf16[2,1024,768]{2,1,0:T(8,128)(2,1)}), bf16[2,256,768]{2,1,0:T(8,128)(2,1)}) %reduce-scatter.11.cloned.1.call-update) | async-done | bytes 786448 | tf_op jit(solution)/shard_map/reduce_scatter | solution.py:168
  436.1 3.6 fusion.107
  442.9 5.6 fusion.79
  453.0 17.5 %all-gather.17.cloned.1.call-done = bf16[2,1024,768]{2,1,0:T(8,128)(2,1)} async-done(((bf16[2,256,768]{2,1,0:T(8,128)(2,1)}), bf16[2,1024,768]{2,1,0:T(8,128)(2,1)}) %all-gather.17.cloned.1.call-update) | async-done | bytes 3145744 | tf_op jit(solution)/shard_map/all_gather | solution.py:196
  470.5 3.1 convolution_convert_fusion
  476.4 64.6 %while.33 = (s32[]{:T(128)}, bf16[4,512,3,64]{1,3,2,0:T(8,128)(2,1)}, f32[4,1024,3,64]{1,3,2,0:T(8,128)}, f32[4,1024,3,64]{1,3,2,0:T(8,128)}, s32[4]{0:T(128)S(1...) while((s32[]{:T(128)}, ...), condition=%wide.region_15.16_spmd, body=%wide.region_13.15_spmd.sunk | while | flops 1031043584 | bytes 59572856 | solution.py:233
  565.2 6.2 bitcast_convert_fusion
  578.4 50.8 %reduce-scatter.19.cloned.1.call-done = bf16[96,768]{1,0:T(8,128)(2,1)} async-done(((bf16[768,768]{1,0:T(8,128)(2,1)}), bf16[96,768]{1,0:T(8,128)(2,1)}) %reduce-scatter.19.cloned.1.call-update) | async-done | bytes 147472
  637.5 31.3 %reduce-scatter.15.cloned.1.call-done = bf16[2,256,768]{2,1,0:T(8,128)(2,1)} async-done(((bf16[2,1024,768]{2,1,0:T(8,128)(2,1)}), bf16[2,256,768]{2,1,0:T(8,128)(2,1)}) %reduce-scatter.15.cloned.1.call-update) | async-done | bytes 786448 | tf_op jit(solution)/shard_map/reduce_scatter | solution.py:252
  671.3 39.7 %psum.7 = f32[12,768]{1,0:T(8,128)S(1)} all-reduce(f32[12,768]{1,0:T(8,128)S(1)} %concatenate.8), channel_id=1, replica_groups=mesh['wide'=8,'narrow'=4] {'wide','narrow'}, use_global_device_ids=true, to_apply=%region_32.33 | all-reduce | flops 9216 | bytes 73728 | tf_op jit(solution)/shard_map/psum | solution.py:290
  (277 shorter events, 164.1 us)
Async XLA Ops:
  7.2 50.5 %all-gather.9.cloned.1.call-start = ((), (), s32[]{:S(2)}) async-start(), calls=%async_computation.7 | async-start | bytes 1769472 | tf_op jit(solution)/shard_map/all_gather | solution.py:85
  9.2 77.4 %all-gather.7.cloned.1.call-start = ((), (), s32[]{:S(2)}) async-start(), calls=%async_computation.6 | async-start | bytes 3932160 | tf_op jit(solution)/shard_map/all_gather | solution.py:89
  9.9 196.2 %reduce-scatter.9.cloned.1.call-start = ((), (), s32[]{:S(2)}) async-start(), calls=%async_computation.8 | async-start | bytes 7864320 | tf_op jit(solution)/shard_map/reduce_scatter | solution.py:155
  11.8 82.1 %copy-start.24 = (f32[768]{0:T(1024)}, f32[768]{0:T(1024)S(1)}, u32[]{:S(2)}) copy-start(f32[768]{0:T(1024)S(1)} %get-tuple-element.520) | copy-start | bytes 9220
  61.5 33.7 %copy-start.16 = (bf16[3,768,192]{1,2,0:T(8,128)(2,1)}, bf16[3,768,192]{1,2,0:T(8,128)(2,1)S(1)}, u32[]{:S(2)}) copy-start(bf16[3,768,192]{1,2,0:T(8,128)(2,1)S(1)} %copy.93) | copy-start | bytes 2654212
  139.3 8.3 %copy-start.3 = (bf16[2,1024,3,64]{1,3,2,0:T(8,128)(2,1)}, bf16[2,1024,3,64]{1,3,2,0:T(8,128)(2,1)S(1)}, u32[]{:S(2)}) copy-start(bf16[2,1024,3,64]{1,3,2,0:T(8,128)(2,1)S(1)} %get-tuple-element.774) | copy-start | bytes 2359300
  141.4 6.2 copy-start.5
  147.6 113.3 %all-gather.13.cloned.1.call-start = ((), (), s32[]{:S(2)}) async-start(), calls=%async_computation.10 | async-start | bytes 2654208 | tf_op jit(solution)/shard_map/all_gather | solution.py:86
  149.4 140.7 %all-gather.11.cloned.1.call-start = ((), (), s32[]{:S(2)}) async-start(), calls=%async_computation.9 | async-start | bytes 3932160 | tf_op jit(solution)/shard_map/all_gather | solution.py:162
  209.6 110.6 %all-gather.15.cloned.1.call-start = ((), (), s32[]{:S(2)}) async-start(), calls=%async_computation.12 | async-start | bytes 3932160 | tf_op jit(solution)/shard_map/all_gather | solution.py:90
  210.2 185.3 %reduce-scatter.13.cloned.1.call-start = ((), (), s32[]{:S(2)}) async-start(), calls=%async_computation.13 | async-start | bytes 7864320 | tf_op jit(solution)/shard_map/reduce_scatter | solution.py:187
  320.2 12.3 %copy-start.30 = (bf16[2,768,768]{2,1,0:T(8,128)(2,1)S(1)}, bf16[2,768,768]{2,1,0:T(8,128)(2,1)}, u32[]{:S(2)}) copy-start(bf16[2,768,768]{2,1,0:T(8,128)(2,1)} %all-gather.13.cloned.1.call-done) | copy-start | bytes 7077892
  337.0 99.1 %reduce-scatter.11.cloned.1.call-start = ((), (), s32[]{:S(2)}) async-start(), calls=%async_computation.11 | async-start | bytes 3932160 | tf_op jit(solution)/shard_map/reduce_scatter | solution.py:168
  343.6 92.4 %copy-start.28 = (f32[768]{0:T(1024)S(1)}, f32[768]{0:T(1024)}, u32[]{:S(2)}) copy-start(f32[768]{0:T(1024)} %get-tuple-element.525) | copy-start | bytes 9220
  343.7 126.8 %all-gather.17.cloned.1.call-start = ((), (), s32[]{:S(2)}) async-start(), calls=%async_computation.14 | async-start | bytes 3932160 | tf_op jit(solution)/shard_map/all_gather | solution.py:196
  441.8 133.1 %reduce-scatter.17.cloned.1.call-start = ((), (), s32[]{:S(2)}) async-start(), calls=%async_computation.16 | async-start | bytes 2654208 | tf_op jit(solution)/shard_map/reduce_scatter | solution.py:297
  452.9 176.3 %reduce-scatter.19.cloned.1.call-start = ((), (), s32[]{:S(2)}) async-start(), calls=%async_computation.17 | async-start | bytes 1327104
  565.1 103.7 %reduce-scatter.15.cloned.1.call-start = ((), (), s32[]{:S(2)}) async-start(), calls=%async_computation.15 | async-start | bytes 3932160 | tf_op jit(solution)/shard_map/reduce_scatter | solution.py:252
  578.2 90.6 %copy-start.25 = (f32[768]{0:T(1024)S(1)}, f32[768]{0:T(1024)}, u32[]{:S(2)}) copy-start(f32[768]{0:T(1024)} %copy-done.24) | copy-start | bytes 9220
  631.4 79.6 %copy-start.23 = (f32[12,768]{1,0:T(8,128)S(1)}, f32[12,768]{1,0:T(8,128)}, u32[]{:S(2)}) copy-start(f32[12,768]{1,0:T(8,128)} %param.25) | copy-start | bytes 110596
  631.4 79.6 %copy-start.26 = (f32[12,768]{1,0:T(8,128)S(1)}, f32[12,768]{1,0:T(8,128)}, u32[]{:S(2)}) copy-start(f32[12,768]{1,0:T(8,128)} %param.26) | copy-start | bytes 110596
  631.4 79.6 %copy-start.27 = (f32[12,768]{1,0:T(8,128)S(1)}, f32[12,768]{1,0:T(8,128)}, u32[]{:S(2)}) copy-start(f32[12,768]{1,0:T(8,128)} %param.27) | copy-start | bytes 110596
  632.6 79.2 %copy-start.2 = (f32[2,256,768]{2,1,0:T(8,128)S(1)}, f32[2,256,768]{2,1,0:T(8,128)}, u32[]{:S(2)}) copy-start(f32[2,256,768]{2,1,0:T(8,128)} %copy-done.1) | copy-start | bytes 4718596
  668.8 43.0 %copy-start.12 = (bf16[2,256,768]{2,1,0:T(8,128)(2,1)S(1)}, bf16[2,256,768]{2,1,0:T(8,128)(2,1)}, u32[]{:S(2)}) copy-start(bf16[2,256,768]{2,1,0:T(8,128)(2,1)} %reduce-scatter.15.cloned.1.call-done) | copy-start | bytes 2359300
  (28 other events, 69.5 us)
Sparse Core Ops, SparseCore 0:
  10.8 46.8 all-gather.8
  59.2 27.3 all-gather.6
  147.8 58.3 reduce-scatter.8
  209.0 51.9 all-gather.12
  263.0 27.0 all-gather.10
  291.6 28.5 all-gather.14
  337.1 58.3 reduce-scatter.12
  398.0 37.9 reduce-scatter.10
  441.9 28.5 all-gather.16
  474.2 69.1 reduce-scatter.16
  565.3 63.9 reduce-scatter.18
  631.8 36.9 reduce-scatter.14
where the time goes:
time: 732 us; the launch traced here: 722 us
  waiting for transfers between devices  409 us (56%)
  matrix products  122 us (17%)
  other arithmetic  54.4 us (7%)
  local copies, waits for them, and re-layouts  53.4 us (7%)
  blocking collectives  39.7 us (5%)
  loops' own time  27.1 us (4%)
  between operations  15.4 us (2%)
    reduce_scatter x1, waiting for transfers between devices, local(): lax.psum_scatter(out_part.reshape(sequence_count, seq_len, width), 'narro...  56.7 us
    unnamed x13, waiting for transfers between devices  52.2 us
    reduce_scatter x1, waiting for transfers between devices, local(): lax.psum_scatter(norm_two_part.reshape(sequence_count, seq_len, width), '...  51.6 us
    all_gather x1, waiting for transfers between devices, local(): lax.all_gather(mlp_w.astype(jnp.bfloat16), 'wide', axis=1, tiled=True)  50.6 us
    all_gather x1, waiting for transfers between devices, local(): lax.all_gather(attn_w.astype(jnp.bfloat16), 'wide', axis=1, tiled=True)  45.8 us
    psum x1, blocking collectives, local(): vec_grad = lax.psum(vec_local, ('wide', 'narrow'))  39.7 us
    reduce_scatter x1, waiting for transfers between devices, local(): lax.psum_scatter(down_part.reshape(sequence_count, seq_len, width).astype...  38.4 us
    reduce_scatter x1, waiting for transfers between devices, local(): lax.psum_scatter(norm_one_part.reshape(sequence_count, seq_len, width).as...  31.3 us
  transfers between devices with their start and end apart: 12, of which 11 were waited for; matrix products, arithmetic and copies ran while one was open for 20% of the time, Pallas kernels for 0%

commit v1 on v0

v1 whole, which is shorter than its diff:
```python
import functools

import jax
import jax.numpy as jnp
from jax import lax
from jax.experimental import pallas as pl
from jax.experimental.pallas import tpu as pltpu
from jax.sharding import PartitionSpec as P

HEAD_DIM = 64
STEP = 10


EPS_NORM = 1e-06
MASKED_SCORE = -1e30
BETA_ONE = 0.5
BETA_TWO = 0.5
EPS_ADAM = 1e-08
RATE_MATRIX = 0.04
RATE_VECTOR = 0.3
DECAY_MATRIX = 0.05
SCALE = HEAD_DIM ** (-0.5)
TILE = 256
F32 = jnp.float32
BF16 = jnp.bfloat16
AXES = ("wide", "narrow")
VMEM_LIMIT = 48 * 1024 * 1024


def adamw_update(weight, first_mom, second, gradient, step_rate, decay_rate):
    first_new = BETA_ONE * first_mom + (1.0 - BETA_ONE) * gradient
    second_new = BETA_TWO * second + (1.0 - BETA_TWO) * gradient * gradient
    corrected = (
        first_new
        / (1.0 - BETA_ONE**STEP)
        / (jnp.sqrt(second_new / (1.0 - BETA_TWO**STEP)) + EPS_ADAM)
    )
    return (weight - step_rate * (corrected + decay_rate * weight), first_new, second_new)


def nn(a, b):
    return lax.dot_general(a, b, (((1,), (0,)), ((), ())), preferred_element_type=F32)


def nt(a, b):
    return lax.dot_general(a, b, (((1,), (1,)), ((), ())), preferred_element_type=F32)


def tn(a, b):
    return lax.dot_general(a, b, (((0,), (0,)), ((), ())), preferred_element_type=F32)


def standardize(v):
    centred = v - jnp.mean(v, axis=-1, keepdims=True)
    inv = lax.rsqrt(jnp.mean(centred * centred, axis=-1, keepdims=True) + EPS_NORM)
    return centred * inv, inv


def norm_back(grad_out, normed, inv, gain):
    scaled = grad_out * gain
    return inv * (
        scaled
        - jnp.mean(scaled, axis=-1, keepdims=True)
        - normed * jnp.mean(scaled * normed, axis=-1, keepdims=True)
    )


def whole(shape):
    return pl.BlockSpec(shape, lambda *_: (0,) * len(shape))


def params(cost=None):
    return pltpu.CompilerParams(
        dimension_semantics=("arbitrary",), vmem_limit_bytes=VMEM_LIMIT
    )


def call(kernel, grid, in_specs, out_specs, out_shape, scratch=(), flops=0, nbytes=0, trans=0):
    return pl.pallas_call(
        kernel,
        grid=grid,
        in_specs=in_specs,
        out_specs=out_specs,
        out_shape=out_shape,
        scratch_shapes=scratch,
        compiler_params=params(),
        cost_estimate=pl.CostEstimate(flops=flops, bytes_accessed=nbytes, transcendentals=trans),
    )


def qkv_kernel(x_ref, gain_ref, shift_ref, w0_ref, w1_ref, bias_ref, a_ref, qkv_ref):
    normed, _ = standardize(x_ref[...].astype(F32))
    low = (normed * gain_ref[...] + shift_ref[...]).astype(BF16)
    a_ref[...] = low
    cols = qkv_ref.shape[2]
    for j, w_ref in enumerate((w0_ref, w1_ref)):
        qkv_ref[j] = (nn(low, w_ref[:, :cols]) + bias_ref[j : j + 1]).astype(BF16)


def attend_kernel(qkv_q_ref, qkv_ref, seg_col_ref, seg_row_ref, w0_ref, w1_ref,
                  ctx_ref, lse_ref, out_ref):
    cols = ctx_ref.shape[2]
    heads = cols // HEAD_DIM
    same = seg_col_ref[...] == seg_row_ref[...]
    lane = lax.broadcasted_iota(jnp.int32, (TILE, 128), 1)
    totals = jnp.zeros((TILE, 128), F32)
    for j in range(2):
        for h in range(heads):
            lo = h * HEAD_DIM
            q = qkv_q_ref[j, :, lo : lo + HEAD_DIM]
            k = qkv_ref[j, :, cols + lo : cols + lo + HEAD_DIM]
            v = qkv_ref[j, :, 2 * cols + lo : 2 * cols + lo + HEAD_DIM]
            s = jnp.where(same, nt(q, k) * SCALE, MASKED_SCORE)
            top = jnp.max(s, axis=-1, keepdims=True)
            e = jnp.exp(s - top)
            total = jnp.sum(e, axis=-1, keepdims=True)
            o = nn(e.astype(BF16), v) / total
            ctx_ref[j, :, lo : lo + HEAD_DIM] = o.astype(BF16)
            totals = jnp.where(lane == j * heads + h, top + jnp.log(total), totals)
    lse_ref[...] = totals.T[: lse_ref.shape[0]]
    acc = nt(ctx_ref[0], w0_ref[:, 3 * cols :]) + nt(ctx_ref[1], w1_ref[:, 3 * cols :])
    out_ref[...] = acc.astype(BF16)


def mlp_kernel(x_ref, p0_ref, p1_ref, dy_ref, vec_ref, bu_ref, u0_ref, u1_ref, d0_ref, d1_ref,
               a_ref, z_ref, du_ref, down_ref, da_ref, gbu_ref):
    @pl.when(pl.program_id(0) == 0)
    def _():
        gbu_ref[...] = jnp.zeros_like(gbu_ref)

    h = x_ref[...].astype(F32) + (p0_ref[...].astype(F32) + p1_ref[...].astype(F32)) + vec_ref[4:5]
    normed, _ = standardize(h)
    a = (normed * vec_ref[2:3] + vec_ref[3:4]).astype(BF16)
    a_ref[...] = a
    dy = dy_ref[...]
    down = jnp.zeros(down_ref.shape, F32)
    da = jnp.zeros(down_ref.shape, F32)
    for j, (u_ref, d_ref) in enumerate(((u0_ref, d0_ref), (u1_ref, d1_ref))):
        u = nn(a, u_ref[...]) + bu_ref[j : j + 1]
        cdf = 0.5 + 0.5 * lax.erf(u * 0.7071067811865476)
        z = (u * cdf).astype(BF16)
        z_ref[j] = z
        slope = cdf + u * (0.3989422804014327 * jnp.exp(-0.5 * u * u))
        du = (nn(dy, d_ref[...]) * slope).astype(BF16)
        du_ref[j] = du
        gbu_ref[j : j + 1] += jnp.sum(du.astype(F32), axis=0, keepdims=True)
        down += nt(z, d_ref[...])
        da += nt(du, u_ref[...])
    down_ref[...] = down.astype(BF16)
    da_ref[...] = da.astype(BF16)


def mid_kernel(x_ref, p0_ref, p1_ref, dy_ref, da0_ref, da1_ref, ctx_ref, vec_ref, w0_ref, w1_ref,
               dh_ref, dctx_ref, delta_ref, sums_ref):
    @pl.when(pl.program_id(0) == 0)
    def _():
        sums_ref[...] = jnp.zeros_like(sums_ref)

    h = x_ref[...].astype(F32) + (p0_ref[...].astype(F32) + p1_ref[...].astype(F32)) + vec_ref[4:5]
    normed, inv = standardize(h)
    da = da0_ref[...].astype(F32) + da1_ref[...].astype(F32)
    dy = dy_ref[...].astype(F32)
    dh = dy + norm_back(da, normed, inv, vec_ref[2:3])
    low = dh.astype(BF16)
    dh_ref[...] = low
    sums_ref[0:1] += jnp.sum(da * normed, axis=0, keepdims=True)
    sums_ref[1:2] += jnp.sum(da, axis=0, keepdims=True)
    sums_ref[2:3] += jnp.sum(dh, axis=0, keepdims=True)
    sums_ref[3:4] += jnp.sum(dy, axis=0, keepdims=True)
    cols = ctx_ref.shape[2]
    heads = cols // HEAD_DIM
    lane = lax.broadcasted_iota(jnp.int32, (TILE, 128), 1)
    deltas = jnp.zeros((TILE, 128), F32)
    for j, w_ref in enumerate((w0_ref, w1_ref)):
        dctx = nn(low, w_ref[:, 3 * cols :]).astype(BF16)
        dctx_ref[j] = dctx
        prod = dctx.astype(F32) * ctx_ref[j].astype(F32)
        for hd in range(heads):
            part = jnp.sum(prod[:, hd * HEAD_DIM : (hd + 1) * HEAD_DIM], axis=-1, keepdims=True)
            deltas = jnp.where(lane == j * heads + hd, part, deltas)
    delta_ref[...] = deltas.T[: delta_ref.shape[0]]


def attend_back_kernel(qkv_ref, dctx_ref, lse_ref, delta_ref, seg_col_ref, seg_row_ref,
                       dqkv_ref, sums_ref, dk_ref, dv_ref):
    j = pl.program_id(0)
    cols = dctx_ref.shape[2]
    heads = cols // HEAD_DIM
    length = qkv_ref.shape[1]
    for h in range(heads):
        lo = h * HEAD_DIM
        k = qkv_ref[0, :, cols + lo : cols + lo + HEAD_DIM]
        v = qkv_ref[0, :, 2 * cols + lo : 2 * cols + lo + HEAD_DIM]
        for t in range(length // TILE):
            rows = slice(t * TILE, (t + 1) * TILE)
            q = qkv_ref[0, rows, lo : lo + HEAD_DIM]
            dc = dctx_ref[0, rows, lo : lo + HEAD_DIM]
            same = seg_col_ref[...] == seg_row_ref[:, rows]
            s = jnp.where(same, nt(k, q) * SCALE, MASKED_SCORE)
            p = jnp.exp(s - lse_ref[0, h : h + 1, rows])
            ds = (p * (nt(v, dc) - delta_ref[0, h : h + 1, rows])).astype(BF16)
            dv = nn(p.astype(BF16), dc)
            dk = nn(ds, q)
            if t == 0:
                dv_ref[...] = dv
                dk_ref[...] = dk
            else:
                dv_ref[...] += dv
                dk_ref[...] += dk
            dqkv_ref[0, rows, lo : lo + HEAD_DIM] = (tn(ds, k) * SCALE).astype(BF16)
        dqkv_ref[0, :, cols + lo : cols + lo + HEAD_DIM] = (dk_ref[...] * SCALE).astype(BF16)
        dqkv_ref[0, :, 2 * cols + lo : 2 * cols + lo + HEAD_DIM] = dv_ref[...].astype(BF16)
    sums_ref[0] = jnp.sum(dqkv_ref[0].astype(F32), axis=0, keepdims=True)


def final_kernel(x_ref, da0_ref, da1_ref, dh_ref, vec_ref, dx_ref, sums_ref):
    @pl.when(pl.program_id(0) == 0)
    def _():
        sums_ref[...] = jnp.zeros_like(sums_ref)

    normed, inv = standardize(x_ref[...].astype(F32))
    da = da0_ref[...].astype(F32) + da1_ref[...].astype(F32)
    dx_ref[...] = dh_ref[...].astype(F32) + norm_back(da, normed, inv, vec_ref[0:1])
    sums_ref[0:1] += jnp.sum(da * normed, axis=0, keepdims=True)
    sums_ref[1:2] += jnp.sum(da, axis=0, keepdims=True)


def local(
    tokens,
    segment_ids,
    cotangent,
    attn_w,
    attn_m,
    attn_v,
    mlp_w,
    mlp_m,
    mlp_v,
    vectors,
    vec_m,
    vec_v,
):
    wide = lax.axis_size("wide")
    narrow = lax.axis_size("narrow")
    widx = lax.axis_index("wide")
    nidx = lax.axis_index("narrow")
    y = nidx // 2
    c = nidx % 2
    other = (1 - y) * 2 + c
    xbit = widx % 2
    first_core = c == 0
    first_y = y == 0
    _, shard_len, width = tokens.shape
    length = segment_ids.shape[1]
    cols = attn_w.shape[2]
    rows = attn_w.shape[1]
    hidden = mlp_w.shape[2]
    heads = cols // HEAD_DIM
    bits = wide.bit_length() - 1
    upper = wide // 2

    def swap(value, partner):
        pairs = [
            (w * narrow + n, (lambda t: t[0] * narrow + t[1])(partner(w, n)))
            for w in range(wide)
            for n in range(narrow)
        ]
        return lax.ppermute(value, AXES, pairs)

    def over_core(value):
        return swap(value, lambda w, n: (w, n ^ 1))

    def over_y(value):
        return swap(value, lambda w, n: (w, n ^ 2))

    def over_bit(value, b):
        return swap(value, lambda w, n: (w ^ (1 << b), n))

    def mixed_one(value):
        return swap(value, lambda w, n: (w ^ 1, n) if n % 2 == 0 else (w, n ^ 2))

    def mixed_two(value):
        return swap(value, lambda w, n: (w ^ 1, n) if n % 2 == 1 else (w, n ^ 2))

    def pair(flag, first, second, axis):
        return jnp.stack(
            [jnp.where(flag, first, second), jnp.where(flag, second, first)], axis=axis
        )

    def gather(shard):
        held = shard[None]
        for b in range(1, bits):
            came = over_bit(held, b)
            high = ((widx >> b) & 1) == 1
            held = jnp.concatenate(
                [jnp.where(high, came, held), jnp.where(high, held, came)], axis=0
            )
        one = mixed_one(held)
        two = mixed_two(jnp.stack([held, one]))
        from_x = jnp.where(first_core, one, two[0])
        from_y = jnp.where(first_core, two[0], one)
        return (held, from_x, from_y, two[1])

    def arrange(pieces, m):
        held, from_x, from_y, diagonal = (p[:, m] for p in pieces)
        even = xbit == 0
        mine = pair(even, held, from_x, 1).reshape(upper * 2 * rows, -1)
        others = pair(even, from_y, diagonal, 1).reshape(upper * 2 * rows, -1)
        return (mine, others)

    def scatter(grads):
        mine = jnp.stack([g[0].astype(BF16) for g in grads]).reshape(-1, upper, 2, rows, width)
        others = jnp.stack([g[1].astype(BF16) for g in grads]).reshape(-1, upper, 2, rows, width)
        even = xbit == 0
        own = jnp.where(even, mine[:, :, 0], mine[:, :, 1])
        to_x = jnp.where(even, mine[:, :, 1], mine[:, :, 0])
        to_y = jnp.where(even, others[:, :, 0], others[:, :, 1])
        diagonal = jnp.where(even, others[:, :, 1], others[:, :, 0])
        came = mixed_two(jnp.stack([jnp.where(first_core, to_y, to_x), diagonal]))
        left = jnp.where(first_core, to_x, to_y).astype(F32) + came[1].astype(F32)
        last = mixed_one(left.astype(BF16))
        total = own.astype(F32) + came[0].astype(F32) + last.astype(F32)
        for b in reversed(range(1, bits)):
            half = total.shape[1] // 2
            high = ((widx >> b) & 1) == 1
            keep = jnp.where(high, total[:, half:], total[:, :half])
            send = jnp.where(high, total[:, :half], total[:, half:])
            total = keep + over_bit(send.astype(BF16), b).astype(F32)
        return total[:, 0]

    def own_row(value):
        keep = jnp.where(first_y, value[0], value[1])
        came = over_y(jnp.where(first_y, value[1], value[0]))
        mine = pair(first_y, keep, came, 0)
        theirs = over_core(mine)
        return pair(first_core, mine, theirs, 1).reshape(length, width)

    def home(value):
        keep = jnp.where(first_y, value[0], value[1])
        send = jnp.where(first_y, value[1], value[0])
        came = over_y(send.astype(BF16)).astype(value.dtype)
        return pair(first_y, keep, came, 0)

    def by_core(value):
        value = value.reshape(2, 2, shard_len, width)
        return (
            jnp.where(first_core, value[:, 0], value[:, 1]),
            jnp.where(first_core, value[:, 1], value[:, 0]),
        )

    def both(vector, size):
        return jnp.stack(
            [
                lax.dynamic_slice_in_dim(vector, nidx * size, size),
                lax.dynamic_slice_in_dim(vector, other * size, size),
            ]
        )

    x_row = own_row(tokens)
    attn_low = attn_w.astype(BF16)
    attn_shard = jnp.concatenate([attn_low[i] for i in range(4)], axis=-1)[None]
    attn_pieces = gather(attn_shard)
    a_mine, a_others = arrange(attn_pieces, 0)
    mlp_pieces = gather(mlp_w.astype(BF16))
    up_mine, up_others = arrange(mlp_pieces, 0)
    down_mine, down_others = arrange(mlp_pieces, 1)
    dy_row = own_row(cotangent)

    seg_own = lax.dynamic_index_in_dim(segment_ids, y, 0, False)
    seg_row = seg_own[None, :]
    seg_col = seg_own[:, None]
    query_bias = both(vectors[6], cols)
    value_bias = both(vectors[7], cols)
    qkv_bias = jnp.concatenate([query_bias, jnp.zeros_like(query_bias), value_bias], axis=1)
    up_bias = both(vectors[8:].reshape(-1), hidden)

    tiles = length // TILE
    full = (TILE, width)
    tile_spec = pl.BlockSpec(full, lambda t: (t, 0))
    weight_spec = whole((width, 4 * cols))
    qkv_cols = 3 * cols
    matmul = 2 * length * width

    normed_low, qkv = call(
        qkv_kernel,
        (tiles,),
        [tile_spec, whole((1, width)), whole((1, width)), weight_spec, weight_spec,
         whole((2, qkv_cols))],
        [tile_spec, pl.BlockSpec((2, TILE, qkv_cols), lambda t: (0, t, 0))],
        [jax.ShapeDtypeStruct((length, width), BF16),
         jax.ShapeDtypeStruct((2, length, qkv_cols), BF16)],
        flops=matmul * 2 * qkv_cols,
        nbytes=10_000_000,
    )(x_row, vectors[0:1], vectors[1:2], a_mine, a_others, qkv_bias)

    ctx_spec = pl.BlockSpec((2, TILE, cols), lambda t: (0, t, 0))
    context, lse, out_part = call(
        attend_kernel,
        (tiles,),
        [pl.BlockSpec((2, TILE, qkv_cols), lambda t: (0, t, 0)), whole((2, length, qkv_cols)),
         pl.BlockSpec((TILE, 1), lambda t: (t, 0)), whole((1, length)), weight_spec, weight_spec],
        [ctx_spec, pl.BlockSpec((8, TILE), lambda t: (0, t)), tile_spec],
        [jax.ShapeDtypeStruct((2, length, cols), BF16), jax.ShapeDtypeStruct((8, length), F32),
         jax.ShapeDtypeStruct((length, width), BF16)],
        flops=2 * matmul * 2 * cols + 4 * length * length * 2 * cols,
        nbytes=12_000_000,
        trans=2 * heads * length * length,
    )(qkv, qkv, seg_col, seg_row, a_mine, a_others)

    out_came = over_core(out_part)

    pair_spec = pl.BlockSpec((2, TILE, hidden), lambda t: (0, t, 0))
    up_spec = whole((width, hidden))
    second_low, activated, grad_pre, down_part, second_part, up_bias_sums = call(
        mlp_kernel,
        (tiles,),
        [tile_spec] * 4 + [whole(vectors.shape), whole((2, hidden))] + [up_spec] * 4,
        [tile_spec, pair_spec, pair_spec, tile_spec, tile_spec, whole((2, hidden))],
        [jax.ShapeDtypeStruct((length, width), BF16),
         jax.ShapeDtypeStruct((2, length, hidden), BF16),
         jax.ShapeDtypeStruct((2, length, hidden), BF16),
         jax.ShapeDtypeStruct((length, width), BF16),
         jax.ShapeDtypeStruct((length, width), BF16),
         jax.ShapeDtypeStruct((2, hidden), F32)],
        flops=4 * matmul * 2 * hidden,
        nbytes=25_000_000,
        trans=4 * length * hidden,
    )(x_row, out_part, out_came, dy_row, vectors, up_bias, up_mine, up_others, down_mine,
      down_others)

    second_came = over_core(second_part)

    def wgrad(left, right):
        return lax.dot_general(left, right, (((0,), (0,)), ((), ())), preferred_element_type=F32)

    grad_up = [wgrad(second_low, grad_pre[j]) for j in range(2)]
    grad_down = [wgrad(dy_row, activated[j]) for j in range(2)]
    mlp_total = scatter([grad_up, grad_down])

    down_keep, down_send = by_core(down_part)
    down_came = over_core(down_send)
    x_own, _ = by_core(x_row)
    out_own, _ = by_core(out_part)
    came_own, _ = by_core(out_came)
    hidden_own = x_own.astype(F32) + (out_own.astype(F32) + came_own.astype(F32)) + vectors[4]
    block_own = hidden_own + (down_keep.astype(F32) + down_came.astype(F32)) + vectors[5]
    block_out = home(block_own.astype(BF16))

    resid_low, grad_ctx, delta, mid_sums = call(
        mid_kernel,
        (tiles,),
        [tile_spec] * 6 + [ctx_spec, whole(vectors.shape), weight_spec, weight_spec],
        [tile_spec, ctx_spec, pl.BlockSpec((8, TILE), lambda t: (0, t)), whole((8, width))],
        [jax.ShapeDtypeStruct((length, width), BF16),
         jax.ShapeDtypeStruct((2, length, cols), BF16),
         jax.ShapeDtypeStruct((8, length), F32),
         jax.ShapeDtypeStruct((8, width), F32)],
        flops=matmul * 2 * cols,
        nbytes=14_000_000,
    )(x_row, out_part, out_came, dy_row, second_part, second_came, context, vectors, a_mine,
      a_others)

    stat_shape = (2, heads, length)
    grad_qkv, qkv_sums = call(
        attend_back_kernel,
        (2,),
        [pl.BlockSpec((1, length, qkv_cols), lambda j: (j, 0, 0)),
         pl.BlockSpec((1, length, cols), lambda j: (j, 0, 0)),
         pl.BlockSpec((1, heads, length), lambda j: (j, 0, 0)),
         pl.BlockSpec((1, heads, length), lambda j: (j, 0, 0)),
         whole((length, 1)), whole((1, length))],
        [pl.BlockSpec((1, length, qkv_cols), lambda j: (j, 0, 0)),
         pl.BlockSpec((1, 1, qkv_cols), lambda j: (j, 0, 0))],
        [jax.ShapeDtypeStruct((2, length, qkv_cols), BF16),
         jax.ShapeDtypeStruct((2, 1, qkv_cols), F32)],
        scratch=[pltpu.VMEM((length, HEAD_DIM), F32), pltpu.VMEM((length, HEAD_DIM), F32)],
        flops=10 * length * length * 2 * cols,
        nbytes=8_000_000,
        trans=2 * heads * length * length,
    )(qkv, grad_ctx, lse[: 2 * heads].reshape(stat_shape), delta[: 2 * heads].reshape(stat_shape),
      seg_col, seg_row)

    norm_one_part = sum(
        lax.dot_general(
            grad_qkv[j], w[:, :qkv_cols], (((1,), (1,)), ((), ())), preferred_element_type=F32
        )
        for j, w in enumerate((a_mine, a_others))
    ).astype(BF16)
    one_keep, one_send = by_core(norm_one_part)
    one_came = over_core(one_send)
    dh_own, _ = by_core(resid_low)

    half_spec = pl.BlockSpec((shard_len, width), lambda t: (t, 0))
    grad_own, one_sums = call(
        final_kernel,
        (2,),
        [half_spec] * 4 + [whole(vectors.shape)],
        [half_spec, whole((8, width))],
        [jax.ShapeDtypeStruct((2 * shard_len, width), F32),
         jax.ShapeDtypeStruct((8, width), F32)],
        nbytes=6_000_000,
    )(x_own.reshape(-1, width), one_keep.reshape(-1, width), one_came.reshape(-1, width),
      dh_own.reshape(-1, width), vectors)
    block_input_gradient = home(grad_own.reshape(2, shard_len, width))

    grad_attn = [
        jnp.concatenate([wgrad(normed_low, grad_qkv[j]), wgrad(resid_low, context[j])], axis=1)
        for j in range(2)
    ]
    attn_total = scatter([grad_attn])[0]

    def spread(pieces, size):
        empty = jnp.zeros((size * narrow,), F32)
        empty = lax.dynamic_update_slice_in_dim(empty, pieces[0], nidx * size, 0)
        return lax.dynamic_update_slice_in_dim(empty, pieces[1], other * size, 0)

    vec_grad = jnp.concatenate(
        [
            one_sums[:2],
            jnp.where(first_core, mid_sums[:4], 0.0),
            spread(qkv_sums[:, 0, :cols], cols)[None],
            spread(qkv_sums[:, 0, 2 * cols :], cols)[None],
            spread(up_bias_sums, hidden).reshape(-1, width),
        ],
        axis=0,
    )
    vec_grad = vec_grad + over_core(vec_grad)
    vec_grad = vec_grad + over_y(vec_grad)
    for b in range(bits):
        vec_grad = vec_grad + over_bit(vec_grad, b)

    attn_grad = jnp.stack([attn_total[:, i * cols : (i + 1) * cols] for i in range(4)])
    mlp_grad = mlp_total
    attn_new, attn_m_new, attn_v_new = adamw_update(
        attn_w, attn_m, attn_v, attn_grad, RATE_MATRIX, DECAY_MATRIX
    )
    mlp_new, mlp_m_new, mlp_v_new = adamw_update(
        mlp_w, mlp_m, mlp_v, mlp_grad, RATE_MATRIX, DECAY_MATRIX
    )
    vec_new, vec_m_new, vec_v_new = adamw_update(vectors, vec_m, vec_v, vec_grad, RATE_VECTOR, 0.0)
    return (
        block_out,
        block_input_gradient,
        attn_grad,
        attn_new,
        attn_m_new,
        attn_v_new,
        mlp_grad,
        mlp_new,
        mlp_m_new,
        mlp_v_new,
        vec_grad,
        vec_new,
        vec_m_new,
        vec_v_new,
    )


def solution(mesh):
    matrix = P(None, "wide", "narrow")
    rows = P("wide", "narrow", None)
    in_specs = (rows, P("wide", None), rows) + (matrix,) * 6 + (P(),) * 3
    out_specs = (rows, rows) + (matrix,) * 8 + (P(),) * 4
    return jax.shard_map(local, mesh=mesh, in_specs=in_specs, out_specs=out_specs, check_vma=False)
```

time: 732 us -> 337 us (0.46)
  waiting for transfers between devices: 409 us -> 143 us
  matrix products: 122 us -> 18.3 us
  Pallas kernels: 0 us -> 73.3 us
  blocking collectives: 39.7 us -> 0 us
  local copies, waits for them, and re-layouts: 53.4 us -> 22.2 us
  starting transfers between devices: 0.66 us -> 28 us
  loops' own time: 27.1 us -> 0 us
  between operations: 15.4 us -> 2.15 us
  other arithmetic: 54.4 us -> 44.6 us
    all_gather x6 -> x0, waiting for transfers between devices: 179 us -> none  [the longest x1 50.6 us: local(): lax.all_gather(mlp_w.astype(jnp.bfloat16), 'wide', axis=1, tiled=True)]
    reduce_scatter x5 -> x0, waiting for transfers between devices: 178 us -> none  [the longest x1 56.7 us: local(): lax.psum_scatter(out_part.reshape(sequence_count, seq_len, width), 'narro...]
    ppermute x0 -> x31, waiting for transfers between devices: none -> 143 us  [swap(): return lax.ppermute(value, AXES, pairs)]
    dot_general x39 -> x10, matrix products: 120 us -> 18.3 us  [the longest x8 15.5 us: wgrad(): lax.dot_general(left, right, (((0,), (0,)), ((), ())), preferred_element_...]
    pallas_call x0 -> x6, Pallas kernels: none -> 73.3 us  [the longest x1 20.8 us: local(): call(attend_back_kernel, (2,), [pl.BlockSpec((1, length, qkv_cols), lambd...]
    unnamed x13 -> x0, waiting for transfers between devices: 52.2 us -> none
    psum x1 -> x0, blocking collectives: 39.7 us -> none  [local(): vec_grad = lax.psum(vec_local, ('wide', 'narrow'))]
    ppermute x0 -> x31, starting transfers between devices: none -> 28 us  [swap(): return lax.ppermute(value, AXES, pairs)]
  transfers between devices with their start and end apart: 12 -> 31, of which waited for: 11 -> 14; matrix products, arithmetic and copies ran while one was open for 20% -> 20% of each run, Pallas kernels for 0% -> 17%
where the time goes in v1:
time: 337 us; the launch traced here: 332 us
  waiting for transfers between devices  143 us (42%)
  Pallas kernels  73.3 us (22%)
  other arithmetic  44.6 us (13%)
  starting transfers between devices  28 us (8%)
  local copies, waits for them, and re-layouts  22.2 us (7%)
  matrix products  18.3 us (5%)
    ppermute x31, waiting for transfers between devices, swap(): return lax.ppermute(value, AXES, pairs)  143 us
    ppermute x31, starting transfers between devices, swap(): return lax.ppermute(value, AXES, pairs)  28 us
    pallas_call x1, Pallas kernels, local(): call(attend_back_kernel, (2,), [pl.BlockSpec((1, length, qkv_cols), lambd...  20.8 us
    pallas_call x1, Pallas kernels, local(): call(attend_kernel, (tiles,), [pl.BlockSpec((2, TILE, qkv_cols), lambda t...  18.6 us
    pallas_call x1, Pallas kernels, local(): call(mlp_kernel, (tiles,), [tile_spec] * 4 + [whole(vectors.shape), whole...  16.1 us
    dot_general x8, matrix products, wgrad(): lax.dot_general(left, right, (((0,), (0,)), ((), ())), preferred_element_...  15.5 us
    unnamed x148, local copies, waits for them, and re-layouts  11.3 us
    pallas_call x1, Pallas kernels, local(): call(mid_kernel, (tiles,), [tile_spec] * 6 + [ctx_spec, whole(vectors.sha...  10 us
  transfers between devices with their start and end apart: 31, of which 14 were waited for; matrix products, arithmetic and copies ran while one was open for 20% of the time, Pallas kernels for 17%

profile of v1, /device:TPU:0, one launch (start us, length us, event | category | flops | bytes accessed | tf_op | source)
XLA Modules:
  0.0 332.0 jit_solution(6129058939435175090)
XLA Ops:
  1.9 3.1 collective-permute-start.9
  9.8 3.0 collective-permute-done.9
  12.9 3.1 collective-permute-start.10
  17.0 23.4 %collective-permute-done.10 = bf16[2,2,96,768]{3,2,1,0:T(8,128)(2,1)S(1)} collective-permute-done((bf16[2,2,96,768]{3,2,1,0:T(8,128)(2,1)S(1)}, bf16[2,2,96,768]{3,2,1,0:T(8,128)(2,1)S(1)}, u32[]{:S(2)}, u32[]{:S(2)}) %collective-permute-start.10) | collective-permute-done | bytes 589856 | tf_op jit(solution)/shard_map/ppermute | solution.py:267
  45.5 12.1 %collective-permute-done.3 = bf16[2,1,96,768]{3,2,1,0:T(8,128)(2,1)} collective-permute-done((bf16[2,1,96,768]{3,2,1,0:T(8,128)(2,1)S(1)}, bf16[2,1,96,768]{3,2,1,0:T(8,128)(2,1)}, u32[]{:S(2)}, u32[]{:S(2)}) %collective-permute-start.3) | collective-permute-done | bytes 294944 | tf_op jit(solution)/shard_map/ppermute | solution.py:267
  64.3 6.3 %collective-permute-done.4 = bf16[4,1,96,768]{3,2,0,1:T(8,128)(2,1)S(1)} collective-permute-done((bf16[4,1,96,768]{3,2,0,1:T(8,128)(2,1)S(1)}, bf16[4,1,96,768]{3,2,0,1:T(8,128)(2,1)S(1)}, u32[]{:S(2)}, u32[]{:S(2)}) %collective-permute-start.4) | collective-permute-done | bytes 589856 | tf_op jit(solution)/shard_map/ppermute | solution.py:267
  75.1 30.1 %collective-permute-done.5 = bf16[2,4,1,96,768]{4,3,1,2,0:T(8,128)(2,1)S(1)} collective-permute-done((bf16[2,4,1,96,768]{4,3,1,2,0:T(8,128)(2,1)S(1)}, bf16[2,4,1,96,768]{4,3,1,2,0:T(8,128)(2,1)S(1)}, u32[]{:S(2)}, u32[]{:S(2)}) %collective-permute-start.5) | collective-permute-done | bytes 1179680 | tf_op jit(solution)/shard_map/ppermute | solution.py:267
  105.6 5.4 %shard_map.227 = (bf16[1024,768]{1,0:T(8,128)(2,1)S(1)}, bf16[2,1024,576]{2,1,0:T(8,128)(2,1)}) custom-call(bf16[1024,768]{1,0:T(8,128)(2,1)S(1)} %bitcast.396, f32[1,768]{1,0:T(1,128)S(1)} %get-tuple-element.128.gain_ref, f32[1,768]{1,0:T(1,128)S(1)} %get-tuple-element.127.shift_ref, bf16[768,768]{1,0:T(8,128)(2,1)S(1)} %bitcast.406, ...), custom_call_target="tpu_custom_call" | custom-call | flops 1811939328 | bytes 10000000 | tf_op jit(solution)/shard_map/pallas_call | solution.py:383
  111.0 18.6 %shard_map.228 = (bf16[2,1024,192]{2,1,0:T(8,128)(2,1)S(1)}, f32[8,1024]{1,0:T(8,128)S(1)}, bf16[1024,768]{1,0:T(8,128)(2,1)S(1)}) custom-call(bf16[2,1024,576]{2,1,0:T(8,128)(2,1)} %get-tuple-element.33.qkv_q_ref.qkv_ref, bf16[2,1024,576]{2,1,0:T(8,128)(2,1)} %get-tuple-element.33.qkv_q_ref.qkv_ref, s32[1024,1]{1,0:T(8,128)S(1)} %copy.50.seg_col_ref, ...), custom_call_target="tpu_custom_call" | custom-call | flops 2818572288 | bytes 12000000 | tf_op jit(solution)/shard_map/pallas_call | solution.py:396
  132.4 2.6 copy.63
  139.9 16.1 %shard_map.229 = (bf16[1024,768]{1,0:T(8,128)(2,1)}, bf16[2,1024,768]{2,1,0:T(8,128)(2,1)}, bf16[2,1024,768]{2,1,0:T(8,128)(2,1)}, bf16[1024,768]{1,0:T(8,128)(2...) custom-call(bf16[1024,768]{1,0:T(8,128)(2,1)} %bitcast.397, bf16[1024,768]{1,0:T(8,128)(2,1)} %copy-done.3, ...), custom_call_target="tpu_custom_call" | custom-call | flops 9663676416 | bytes 25000000 | tf_op jit(solution)/shard_map/pallas_call | solution.py:413
  156.0 4.6 %fusion.28 = bf16[768,768]{1,0:T(8,128)(2,1)} fusion(bf16[1024,768]{1,0:T(8,128)(2,1)} %get-tuple-element.45, bf16[2,1024,768]{2,1,0:T(8,128)(2,1)} %get-tuple-element.46), kind=kOutput, calls=%fused_computation.38 | convolution fusion | flops 1208549376 | bytes 4325376 | tf_op jit(solution)/shard_map/dot_general | solution.py:433
  165.8 2.5 fusion.31
  174.9 4.1 %fusion.4 = (bf16[2,256,768]{2,1,0:T(8,128)(2,1)S(1)}, bf16[2,256,768]{2,1,0:T(8,128)(2,1)}) fusion(bf16[2,256,768]{2,1,0:T(8,128)(2,1)} %collective-permute-done.13, bf16[2,2,256,768]{3,2,1,0:T(8,128)(2,1)} %bitcast.23, bf16[2,2,256,768]{3,2,1,0:T(8,128)(2,1)S(1)} %bitcast.401, f32[768]{0:T(1024)S(1)} %copy-done.70, f32[768]{0:T(1024)S(1)} %get-tuple-element.52, ...), kind=kLoop, calls=%fused_computation.17 | loop fusion | flops 7471104 | bytes 8657920 | tf_op jit(solution)/shard_map/convert_element_type | solution.py:446
  180.7 10.0 %shard_map.230 = (bf16[1024,768]{1,0:T(8,128)(2,1)S(1)}, bf16[2,1024,192]{2,1,0:T(8,128)(2,1)S(1)}, f32[8,1024]{1,0:T(8,128)S(1)}, f32[8,768]{1,0:T(8,128)S(1)}) custom-call(bf16[1024,768]{1,0:T(8,128)(2,1)} %bitcast.398, bf16[1024,768]{1,0:T(8,128)(2,1)} %copy-done.3, bf16[1024,768]{1,0:T(8,128)(2,1)} %collective-permute-done.6.p1_ref, ...), custom_call_target="tpu_custom_call" | custom-call | flops 603979776 | bytes 14000000 | tf_op jit(solution)/shard_map/pallas_call | solution.py:448
  193.6 20.8 %shard_map.231 = (bf16[2,1024,576]{2,1,0:T(8,128)(2,1)S(1)}, f32[2,1,576]{2,1,0:T(1,128)S(1)}) custom-call(bf16[2,1024,576]{2,1,0:T(8,128)(2,1)} %get-tuple-element.33.qkv_q_ref.qkv_ref, bf16[2,1024,192]{2,1,0:T(8,128)(2,1)S(1)} %copy-done.24, f32[2,3,1024]{2,1,0:T(4,128)S(1)} %copy-done.20, f32[2,3,1024]{2,1,0:T(4,128)S(1)} %reshape.540.delta_ref, ...), custom_call_target="tpu_custom_call" | custom-call | flops 4026531840 | bytes 8000000 | tf_op jit(solution)/shard_map/pallas_call | solution.py:463
  239.7 8.3 %collective-permute-done.27 = f32[12,768]{1,0:T(8,128)S(1)} collective-permute-done((f32[12,768]{1,0:T(8,128)S(1)}, f32[12,768]{1,0:T(8,128)S(1)}, u32[]{:S(2)}, u32[]{:S(2)}) %collective-permute-start.27) | collective-permute-done | bytes 36896 | tf_op jit(solution)/shard_map/ppermute | solution.py:267
  249.4 3.3 %fusion = bf16[2,4,96,768]{3,2,1,0:T(8,128)(2,1)S(1)} fusion(bf16[2,2,4,96,768]{4,3,2,1,0:T(8,128)(2,1)} %collective-permute-done.22, pred[]{:T(512)S(6)} %eq.14, pred[]{:T(512)S(6)} %eq.15, bf16[1,4,2,96,768]{4,3,2,1,0:T(8,128)(2,1)} %bitcast.424, bf16[1,4,2,96,768]{4,3,2,1,0:T(8,128)(2,1)} %bitcast.421, bf16[1,4,2,96,768]{4,3,2,1,0:T(8,128)(2,1)} %bitcast.436, ...), kind=kLoop, calls=%fused_computation.8 | loop fusion | flops 6488064 | bytes 7077890 | tf_op jit(solution)/shard_map/convert_element_type | solution.py:320
  254.8 2.9 collective-permute-done.29
  265.9 9.5 %collective-permute-done.19 = bf16[1,4,96,768]{3,2,1,0:T(8,128)(2,1)S(1)} collective-permute-done((bf16[1,4,96,768]{3,2,1,0:T(8,128)(2,1)S(1)}, bf16[1,4,96,768]{3,2,1,0:T(8,128)(2,1)S(1)}, u32[]{:S(2)}, u32[]{:S(2)}) %collective-permute-start.19) | collective-permute-done | bytes 589856 | tf_op jit(solution)/shard_map/ppermute | solution.py:267
  279.3 2.9 collective-permute-start.24
  282.2 22.8 %collective-permute-done.20 = bf16[1,2,96,768]{3,2,1,0:T(8,128)(2,1)S(1)} collective-permute-done((bf16[1,2,96,768]{3,2,1,0:T(8,128)(2,1)S(1)}, bf16[1,2,96,768]{3,2,1,0:T(8,128)(2,1)S(1)}, u32[]{:S(2)}, u32[]{:S(2)}) %collective-permute-start.20) | collective-permute-done | bytes 294944 | tf_op jit(solution)/shard_map/ppermute | solution.py:267
  306.5 14.3 %collective-permute-done.21 = bf16[1,1,96,768]{3,2,1,0:T(8,128)(2,1)S(1)} collective-permute-done((bf16[1,1,96,768]{3,2,1,0:T(8,128)(2,1)S(1)}, bf16[1,1,96,768]{3,2,1,0:T(8,128)(2,1)S(1)}, u32[]{:S(2)}, u32[]{:S(2)}) %collective-permute-start.21) | collective-permute-done | bytes 147488 | tf_op jit(solution)/shard_map/ppermute | solution.py:267
  323.5 6.6 %collective-permute-done.25 = bf16[2,1,96,768]{3,2,1,0:T(8,128)(2,1)S(1)} collective-permute-done((bf16[2,1,96,768]{3,2,1,0:T(8,128)(2,1)S(1)}, bf16[2,1,96,768]{3,2,1,0:T(8,128)(2,1)S(1)}, u32[]{:S(2)}, u32[]{:S(2)}) %collective-permute-start.25) | collective-permute-done | bytes 294944 | tf_op jit(solution)/shard_map/ppermute | solution.py:267
  (304 shorter events, 93.5 us)
Async XLA Ops:
  1.9 10.9 %collective-permute-start.9 = (bf16[1,2,96,768]{3,2,1,0:T(8,128)(2,1)S(1)}, bf16[1,2,96,768]{3,2,1,0:T(8,128)(2,1)S(1)}, u32[]{:S(2)}, u32[]{:S(2)}) collective-permute-start(bf16[1,2,96,768]{3,2,1,0:T(8,128)(2,1)S(1)} %convert_bitcast_fusion), channel_id=1, source_target_pairs={{0,8},{1,9},{2,10},{3,11},{4,12},{5,13},{6,14},{7,15},{8,0},{9,1},... | collective-permute-start | bytes 884744 | tf_op jit(solution)/shard_map/ppermute | solution.py:267
  6.8 10.1 %collective-permute-start.2 = (bf16[1,1,96,768]{3,2,1,0:T(8,128)(2,1)}, bf16[1,1,96,768]{3,2,1,0:T(8,128)(2,1)S(1)}, u32[]{:S(2)}, u32[]{:S(2)}) collective-permute-start(bf16[1,1,96,768]{3,2,1,0:T(8,128)(2,1)} %maximum_bitcast_fusion), channel_id=1, source_target_pairs={{0,8},{1,9},{2,10},{3,11},{4,12},{5,13},{6,14},{7,15},{8,0},{9,1},... | collective-permute-start | bytes 442376 | tf_op jit(solution)/shard_map/ppermute | solution.py:267
  6.9 37.2 %collective-permute-start = (bf16[256,768]{1,0:T(8,128)(2,1)S(1)}, bf16[256,768]{1,0:T(8,128)(2,1)}, u32[]{:S(2)}, u32[]{:S(2)}) collective-permute-start(bf16[256,768]{1,0:T(8,128)(2,1)S(1)} %select_bitcast_fusion.9), channel_id=1, source_target_pairs={{0,2},{1,3},{2,0},{3,1},{4,6},{5,7},{6,4},{7,5},{8,10},{9,11},{10,... | collective-permute-start | bytes 1179656 | tf_op jit(solution)/shard_map/ppermute | solution.py:267
  9.6 50.8 %collective-permute-start.7 = (bf16[256,768]{1,0:T(8,128)(2,1)}, bf16[256,768]{1,0:T(8,128)(2,1)}, u32[]{:S(2)}, u32[]{:S(2)}) collective-permute-start(bf16[256,768]{1,0:T(8,128)(2,1)} %select_bitcast_fusion.8), channel_id=1, source_target_pairs={{0,2},{1,3},{2,0},{3,1},{4,6},{5,7},{6,4},{7,5},{8,10},{9,11},{10,... | collective-permute-start | bytes 1179656 | tf_op jit(solution)/shard_map/ppermute | solution.py:267
  12.9 27.4 %collective-permute-start.10 = (bf16[2,2,96,768]{3,2,1,0:T(8,128)(2,1)S(1)}, bf16[2,2,96,768]{3,2,1,0:T(8,128)(2,1)S(1)}, u32[]{:S(2)}, u32[]{:S(2)}) collective-permute-start(bf16[2,2,96,768]{3,2,1,0:T(8,128)(2,1)S(1)} %pad_maximum_fusion.22), channel_id=1, source_target_pairs={{0,16},{1,17},{2,18},{3,19},{4,20},{5,21},{6,22},{7,23},{8,24},{9,... | collective-permute-start | bytes 1769480 | tf_op jit(solution)/shard_map/ppermute | solution.py:267
  42.2 19.4 %collective-permute-start.11 = (bf16[4,2,96,768]{3,2,1,0:T(8,128)(2,1)}, bf16[4,2,96,768]{3,2,1,0:T(8,128)(2,1)S(1)}, u32[]{:S(2)}, u32[]{:S(2)}) collective-permute-start(bf16[4,2,96,768]{3,2,1,0:T(8,128)(2,1)} %get-tuple-element.102), channel_id=1, source_target_pairs={{0,4},{1,3},{2,6},{3,1},{4,0},{5,7},{6,2},{7,5},{8,12},{9,11},{10,... | collective-permute-start | bytes 3538952 | tf_op jit(solution)/shard_map/ppermute | solution.py:267
  43.6 14.0 %collective-permute-start.3 = (bf16[2,1,96,768]{3,2,1,0:T(8,128)(2,1)S(1)}, bf16[2,1,96,768]{3,2,1,0:T(8,128)(2,1)}, u32[]{:S(2)}, u32[]{:S(2)}) collective-permute-start(bf16[2,1,96,768]{3,2,1,0:T(8,128)(2,1)S(1)} %pad_maximum_fusion.24), channel_id=1, source_target_pairs={{0,16},{1,17},{2,18},{3,19},{4,20},{5,21},{6,22},{7,23},{8,24},{9,... | collective-permute-start | bytes 884744 | tf_op jit(solution)/shard_map/ppermute | solution.py:267
  58.7 11.9 %collective-permute-start.4 = (bf16[4,1,96,768]{3,2,0,1:T(8,128)(2,1)S(1)}, bf16[4,1,96,768]{3,2,0,1:T(8,128)(2,1)S(1)}, u32[]{:S(2)}, u32[]{:S(2)}) collective-permute-start(bf16[4,1,96,768]{3,2,0,1:T(8,128)(2,1)S(1)} %get-tuple-element.112), channel_id=1, source_target_pairs={{0,4},{1,3},{2,6},{3,1},{4,0},{5,7},{6,2},{7,5},{8,12},{9,11},{10,... | collective-permute-start | bytes 1769480 | tf_op jit(solution)/shard_map/ppermute | solution.py:267
  60.4 11.9 %collective-permute-start.1 = (bf16[2,256,768]{2,1,0:T(8,128)(2,1)S(1)}, bf16[2,256,768]{2,1,0:T(8,128)(2,1)S(1)}, u32[]{:S(2)}, u32[]{:S(2)}) collective-permute-start(bf16[2,256,768]{2,1,0:T(8,128)(2,1)S(1)} %pad_maximum_fusion.16), channel_id=1, source_target_pairs={{0,1},{1,0},{2,3},{3,2},{4,5},{5,4},{6,7},{7,6},{8,9},{9,8},{10,11... | collective-permute-start | bytes 2359304 | tf_op jit(solution)/shard_map/ppermute | solution.py:267
  63.5 71.6 %collective-permute-start.12 = (bf16[2,4,2,96,768]{4,3,2,1,0:T(8,128)(2,1)}, bf16[2,4,2,96,768]{4,3,2,1,0:T(8,128)(2,1)}, u32[]{:S(2)}, u32[]{:S(2)}) collective-permute-start(bf16[2,4,2,96,768]{4,3,2,1,0:T(8,128)(2,1)} %pad_maximum_fusion), channel_id=1, source_target_pairs={{0,2},{1,5},{2,0},{3,7},{4,6},{5,1},{6,4},{7,3},{8,10},{9,13},{10,... | collective-permute-start | bytes 7077896 | tf_op jit(solution)/shard_map/ppermute | solution.py:267
  70.7 34.5 %collective-permute-start.5 = (bf16[2,4,1,96,768]{4,3,1,2,0:T(8,128)(2,1)S(1)}, bf16[2,4,1,96,768]{4,3,1,2,0:T(8,128)(2,1)S(1)}, u32[]{:S(2)}, u32[]{:S(2)}) collective-permute-start(bf16[2,4,1,96,768]{4,3,1,2,0:T(8,128)(2,1)S(1)} %pad_maximum_fusion.8), channel_id=1, source_target_pairs={{0,2},{1,5},{2,0},{3,7},{4,6},{5,1},{6,4},{7,3},{8,10},{9,13},{10,... | collective-permute-start | bytes 3538952 | tf_op jit(solution)/shard_map/ppermute | solution.py:267
  162.0 18.6 %collective-permute-start.15 = (bf16[1024,768]{1,0:T(8,128)(2,1)}, bf16[1024,768]{1,0:T(8,128)(2,1)}, u32[]{:S(2)}, u32[]{:S(2)}) collective-permute-start(bf16[1024,768]{1,0:T(8,128)(2,1)} %get-tuple-element.36.da0_ref), channel_id=1, source_target_pairs={{0,1},{1,0},{2,3},{3,2},{4,5},{5,4},{6,7},{7,6},{8,9},{9,8},{10,11... | collective-permute-start | bytes 4718600 | tf_op jit(solution)/shard_map/ppermute | solution.py:267
  163.2 11.5 %collective-permute-start.13 = (bf16[2,256,768]{2,1,0:T(8,128)(2,1)}, bf16[2,256,768]{2,1,0:T(8,128)(2,1)}, u32[]{:S(2)}, u32[]{:S(2)}) collective-permute-start(bf16[2,256,768]{2,1,0:T(8,128)(2,1)} %select_bitcast_fusion.3), channel_id=1, source_target_pairs={{0,1},{1,0},{2,3},{3,2},{4,5},{5,4},{6,7},{7,6},{8,9},{9,8},{10,11... | collective-permute-start | bytes 2359304 | tf_op jit(solution)/shard_map/ppermute | solution.py:267
  173.7 75.8 %collective-permute-start.22 = (bf16[2,2,4,96,768]{4,3,2,1,0:T(8,128)(2,1)}, bf16[2,2,4,96,768]{4,3,2,1,0:T(8,128)(2,1)}, u32[]{:S(2)}, u32[]{:S(2)}) collective-permute-start(bf16[2,2,4,96,768]{4,3,2,1,0:T(8,128)(2,1)} %pad_maximum_fusion.1), channel_id=1, source_target_pairs={{0,2},{1,5},{2,0},{3,7},{4,6},{5,1},{6,4},{7,3},{8,10},{9,13},{10,... | collective-permute-start | bytes 7077896 | tf_op jit(solution)/shard_map/ppermute | solution.py:267
  179.7 58.6 %collective-permute-start.14 = (bf16[256,768]{1,0:T(8,128)(2,1)}, bf16[256,768]{1,0:T(8,128)(2,1)}, u32[]{:S(2)}, u32[]{:S(2)}) collective-permute-start(bf16[256,768]{1,0:T(8,128)(2,1)} %select_bitcast_fusion.7), channel_id=1, source_target_pairs={{0,2},{1,3},{2,0},{3,1},{4,6},{5,7},{6,4},{7,5},{8,10},{9,11},{10,... | collective-permute-start | bytes 1179656 | tf_op jit(solution)/shard_map/ppermute | solution.py:267
  222.8 9.6 %collective-permute-start.16 = (bf16[2,256,768]{2,1,0:T(8,128)(2,1)}, bf16[2,256,768]{2,1,0:T(8,128)(2,1)}, u32[]{:S(2)}, u32[]{:S(2)}) collective-permute-start(bf16[2,256,768]{2,1,0:T(8,128)(2,1)} %get-tuple-element.93), channel_id=1, source_target_pairs={{0,1},{1,0},{2,3},{3,2},{4,5},{5,4},{6,7},{7,6},{8,9},{9,8},{10,11... | collective-permute-start | bytes 2359304 | tf_op jit(solution)/shard_map/ppermute | solution.py:267
  230.4 27.4 %collective-permute-start.18 = (bf16[2,1,4,96,768]{4,3,2,1,0:T(8,128)(2,1)}, bf16[2,1,4,96,768]{4,3,2,1,0:T(8,128)(2,1)}, u32[]{:S(2)}, u32[]{:S(2)}) collective-permute-start(bf16[2,1,4,96,768]{4,3,2,1,0:T(8,128)(2,1)} %pad_maximum_fusion.15), channel_id=1, source_target_pairs={{0,2},{1,5},{2,0},{3,7},{4,6},{5,1},{6,4},{7,3},{8,10},{9,13},{10,... | collective-permute-start | bytes 3538952 | tf_op jit(solution)/shard_map/ppermute | solution.py:267
  237.4 10.5 %collective-permute-start.27 = (f32[12,768]{1,0:T(8,128)S(1)}, f32[12,768]{1,0:T(8,128)S(1)}, u32[]{:S(2)}, u32[]{:S(2)}) collective-permute-start(f32[12,768]{1,0:T(8,128)S(1)} %add.219), channel_id=1, source_target_pairs={{0,2},{1,3},{2,0},{3,1},{4,6},{5,7},{6,4},{7,5},{8,10},{9,11},{10,... | collective-permute-start | bytes 110600 | tf_op jit(solution)/shard_map/ppermute | solution.py:267
  252.8 24.3 %collective-permute-start.23 = (bf16[2,4,96,768]{3,2,1,0:T(8,128)(2,1)S(1)}, bf16[2,4,96,768]{3,2,1,0:T(8,128)(2,1)S(1)}, u32[]{:S(2)}, u32[]{:S(2)}) collective-permute-start(bf16[2,4,96,768]{3,2,1,0:T(8,128)(2,1)S(1)} %fusion), channel_id=1, source_target_pairs={{0,4},{1,3},{2,6},{3,1},{4,0},{5,7},{6,2},{7,5},{8,12},{9,11},{10,... | collective-permute-start | bytes 3538952 | tf_op jit(solution)/shard_map/ppermute | solution.py:267
  253.7 12.1 %collective-permute-start.17 = (bf16[256,768]{1,0:T(8,128)(2,1)S(1)}, bf16[256,768]{1,0:T(8,128)(2,1)S(1)}, u32[]{:S(2)}, u32[]{:S(2)}) collective-permute-start(bf16[256,768]{1,0:T(8,128)(2,1)S(1)} %select_convert_fusion.1), channel_id=1, source_target_pairs={{0,2},{1,3},{2,0},{3,1},{4,6},{5,7},{6,4},{7,5},{8,10},{9,11},{10,... | collective-permute-start | bytes 1179656 | tf_op jit(solution)/shard_map/ppermute | solution.py:267
  259.5 15.9 %collective-permute-start.19 = (bf16[1,4,96,768]{3,2,1,0:T(8,128)(2,1)S(1)}, bf16[1,4,96,768]{3,2,1,0:T(8,128)(2,1)S(1)}, u32[]{:S(2)}, u32[]{:S(2)}) collective-permute-start(bf16[1,4,96,768]{3,2,1,0:T(8,128)(2,1)S(1)} %fusion.59), channel_id=1, source_target_pairs={{0,4},{1,3},{2,6},{3,1},{4,0},{5,7},{6,2},{7,5},{8,12},{9,11},{10,... | collective-permute-start | bytes 1769480 | tf_op jit(solution)/shard_map/ppermute | solution.py:267
  277.0 28.0 %collective-permute-start.20 = (bf16[1,2,96,768]{3,2,1,0:T(8,128)(2,1)S(1)}, bf16[1,2,96,768]{3,2,1,0:T(8,128)(2,1)S(1)}, u32[]{:S(2)}, u32[]{:S(2)}) collective-permute-start(bf16[1,2,96,768]{3,2,1,0:T(8,128)(2,1)S(1)} %select_convert_fusion.3), channel_id=1, source_target_pairs={{0,16},{1,17},{2,18},{3,19},{4,20},{5,21},{6,22},{7,23},{8,24},{9,... | collective-permute-start | bytes 884744 | tf_op jit(solution)/shard_map/ppermute | solution.py:267
  279.3 41.5 %collective-permute-start.24 = (bf16[2,2,96,768]{3,2,1,0:T(8,128)(2,1)S(1)}, bf16[2,2,96,768]{3,2,1,0:T(8,128)(2,1)S(1)}, u32[]{:S(2)}, u32[]{:S(2)}) collective-permute-start(bf16[2,2,96,768]{3,2,1,0:T(8,128)(2,1)S(1)} %select_convert_fusion), channel_id=1, source_target_pairs={{0,16},{1,17},{2,18},{3,19},{4,20},{5,21},{6,22},{7,23},{8,24},{9,... | collective-permute-start | bytes 1769480 | tf_op jit(solution)/shard_map/ppermute | solution.py:267
  305.1 15.6 %collective-permute-start.21 = (bf16[1,1,96,768]{3,2,1,0:T(8,128)(2,1)S(1)}, bf16[1,1,96,768]{3,2,1,0:T(8,128)(2,1)S(1)}, u32[]{:S(2)}, u32[]{:S(2)}) collective-permute-start(bf16[1,1,96,768]{3,2,1,0:T(8,128)(2,1)S(1)} %select_convert_fusion.4), channel_id=1, source_target_pairs={{0,8},{1,9},{2,10},{3,11},{4,12},{5,13},{6,14},{7,15},{8,0},{9,1},... | collective-permute-start | bytes 442376 | tf_op jit(solution)/shard_map/ppermute | solution.py:267
  (82 other events, 459.8 us)
